TPU v7x, 32 devices: a whole 2x2x4 slice. The times are simulated.
32 devices in a mesh: dp: 4 (over x, core), expert: 8 (over z, y).
Axes of the slice: x: 2, y: 2, z: 4, core: 2. Of those that a mesh axis runs over, the one named last changes fastest.
Arguments:
- tokens: bfloat16 [2048, 2048], P(('dp', 'expert')), may hold values from -6 to 6
- gate_values: float32 [2048, 4], P(('dp', 'expert')), may hold values from 0.1 to 1
- chosen: int32 [2048, 4], P(('dp', 'expert')), may hold values from 0 to 63, all different within a row; in each aligned block of 64 rows (0 to 63, 64 to 127, ...) at most 8 rows name the same one
- slot_table: int32 [64], replicated, may hold values from 0 to 63, each once
- w_gate: bfloat16 [64, 768, 2048], P('expert', 'dp'), may hold values from -0.125 to 0.125
- w_up: bfloat16 [64, 768, 2048], P('expert', 'dp'), may hold values from -0.125 to 0.125
- w_down: bfloat16 [64, 768, 2048], P('expert', 'dp'), may hold values from -0.21875 to 0.21875
- cotangent: bfloat16 [2048, 2048], P(('dp', 'expert')), may hold values from -0.59765625 to 0.59765625
Outputs:
- mixed: bfloat16 [2048, 2048], P(('dp', 'expert'))
- token_grads: bfloat16 [2048, 2048], P(('dp', 'expert'))
- gate_grads: float32 [2048, 4], P(('dp', 'expert'))
- gate_weight_grad: bfloat16 [64, 768, 2048], P('expert', 'dp')
- up_weight_grad: bfloat16 [64, 768, 2048], P('expert', 'dp')
- down_weight_grad: bfloat16 [64, 768, 2048], P('expert', 'dp')
Inputs may be any that keep to these rules, and one draw needn't show every extreme that they name: `chosen`: each row names 4 distinct experts. Within the rows of one device (aligned blocks of 64 tokens) no expert is named by more than 8 rows, and in every draw some expert is named by exactly 8 rows of some block. `slot_table`: A permutation of the storage indices.
All inputs are finite; a program needn't handle non-finite values.
Results may differ from a plain program's by a relative error of at most 0.009.
Values may be sent and summed in bfloat16 or wider, within the bound.
A program may use at most 384 MiB of HBM per device.

v0:
```python
import jax
import jax.numpy as jnp
from jax import lax
from jax.sharding import PartitionSpec as P

CAP = 8
PAD = 128
F32 = jnp.float32
BF16 = jnp.bfloat16
AXES = ("dp", "expert")


def split3(v):
    a = lax.reduce_precision(v, 8, 7)
    r = v - a
    b = lax.reduce_precision(r, 8, 7)
    return (a.astype(BF16), b.astype(BF16), (r - b).astype(BF16))


def per_device(tokens, gate_values, chosen, slot_table, w_gate, w_up, w_down, cotangent):
    tok, width = tokens.shape
    topk = chosen.shape[1]
    experts = slot_table.shape[0]
    groups = lax.axis_size("expert")
    n_dev = groups * lax.axis_size("dp")
    per_dev = w_gate.shape[0]
    blocks = max(1, min(n_dev, 256 // tok))
    chunks = n_dev // blocks
    labels = jnp.arange(experts, dtype=jnp.int32)
    slot = jnp.sum(jnp.where(chosen[:, :, None] == labels, slot_table, 0), axis=2)
    named = jnp.sum((slot[:, :, None] == labels).astype(F32), axis=1)
    lower = (jnp.arange(tok)[:, None] > jnp.arange(tok)[None, :]).astype(F32)
    before = jnp.dot(lower, named, preferred_element_type=F32)
    pos = jnp.sum(jnp.where(slot[:, :, None] == labels, before[:, None, :], 0.0), axis=2)
    g1, g2, g3 = split3(gate_values)
    extra = jnp.concatenate([slot.astype(BF16), pos.astype(BF16), g1, g2, g3], axis=1)
    extra = jnp.pad(extra, ((0, 0), (0, PAD - extra.shape[1])))
    packed = jnp.concatenate([tokens, cotangent, extra], axis=1)
    allp = lax.all_gather(packed, AXES, axis=0, tiled=True)
    allp = allp.reshape(chunks, blocks * tok, 2 * width + PAD)
    x_all = allp[:, :, :width]
    c_all = allp[:, :, width : 2 * width]
    ex = allp[:, :, 2 * width : 2 * width + 5 * topk].astype(F32)
    ex = ex.reshape(chunks, blocks * tok, 5, topk)
    slot_all = ex[:, :, 0].astype(jnp.int32) - lax.axis_index("expert") * per_dev
    pos_all = ex[:, :, 1].astype(jnp.int32)
    gate_all = ex[:, :, 2] + ex[:, :, 3] + ex[:, :, 4]
    blk = (jnp.arange(blocks * tok, dtype=jnp.int32) // tok)[None, :, None]
    rows = blocks * CAP
    here = (slot_all >= 0) & (slot_all < per_dev)
    row_id = jnp.where(here, slot_all * rows + blk * CAP + pos_all, -1)
    rid = jnp.arange(per_dev * rows, dtype=jnp.int32)[None, :, None, None]
    match = row_id[:, None, :, :] == rid
    sel = jnp.sum(match.astype(F32), axis=3).astype(BF16)
    gate_row = jnp.sum(jnp.where(match, gate_all[:, None], 0.0), axis=(2, 3))

    def to_expert(v):
        v = v.reshape((chunks, per_dev, rows) + v.shape[2:])
        v = jnp.swapaxes(v, 0, 1)
        return v.reshape((per_dev, chunks * rows) + v.shape[3:])

    def to_chunk(v):
        v = v.reshape((per_dev, chunks, rows) + v.shape[2:])
        v = jnp.swapaxes(v, 0, 1)
        return v.reshape((chunks, per_dev * rows) + v.shape[3:])

    x_rows = to_expert(
        jnp.einsum("crt,ctd->crd", sel, x_all, preferred_element_type=F32).astype(BF16)
    )
    c_rows = to_expert(
        jnp.einsum("crt,ctd->crd", sel, c_all, preferred_element_type=F32).astype(BF16)
    )
    gate_e = to_expert(gate_row)[:, :, None]
    pre_gate = jnp.einsum("erd,efd->erf", x_rows, w_gate, preferred_element_type=F32)
    pre_up = jnp.einsum("erd,efd->erf", x_rows, w_up, preferred_element_type=F32)
    dh = jnp.einsum("erd,efd->erf", c_rows, w_down, preferred_element_type=F32)
    s = jax.nn.sigmoid(pre_gate)
    act = pre_gate * s
    hid = act * pre_up
    gg_row = jnp.sum(hid * dh, axis=2)
    hid = (hid * gate_e).astype(BF16)
    dh = dh * gate_e
    grad_gate = (dh * pre_up * s * (1.0 + pre_gate * (1.0 - s))).astype(BF16)
    grad_up = (dh * act).astype(BF16)
    out_rows = jnp.einsum("erf,efd->erd", hid, w_down, preferred_element_type=F32).astype(BF16)
    back_rows = (
        jnp.einsum("erf,efd->erd", grad_gate, w_gate, preferred_element_type=F32)
        + jnp.einsum("erf,efd->erd", grad_up, w_up, preferred_element_type=F32)
    ).astype(BF16)
    dw_gate = jnp.einsum("erf,erd->efd", grad_gate, x_rows, preferred_element_type=F32).astype(BF16)
    dw_up = jnp.einsum("erf,erd->efd", grad_up, x_rows, preferred_element_type=F32).astype(BF16)
    dw_down = jnp.einsum("erf,erd->efd", hid, c_rows, preferred_element_type=F32).astype(BF16)
    part_m = jnp.einsum("crt,crd->ctd", sel, to_chunk(out_rows), preferred_element_type=F32)
    part_b = jnp.einsum("crt,crd->ctd", sel, to_chunk(back_rows), preferred_element_type=F32)
    gg_c = to_chunk(gg_row)
    part_g = jnp.sum(jnp.where(match, gg_c[:, :, None, None], 0.0), axis=1)
    part_g = jnp.pad(part_g, ((0, 0), (0, 0), (0, PAD - topk)))
    part = jnp.concatenate([part_m.astype(BF16), part_b.astype(BF16), part_g.astype(BF16)], axis=2)
    part = part.reshape(n_dev * tok, 2 * width + PAD)
    red = lax.psum_scatter(part, AXES, scatter_dimension=0, tiled=True)
    return (
        red[:, :width],
        red[:, width : 2 * width],
        red[:, 2 * width : 2 * width + topk].astype(F32),
        dw_gate,
        dw_up,
        dw_down,
    )


def solution(mesh):
    tok = P(AXES, None)
    w = P("expert", "dp", None)
    return jax.shard_map(
        per_device,
        mesh=mesh,
        in_specs=(tok, tok, tok, P(), w, w, w, tok),
        out_specs=(tok, tok, tok, w, w, w),
        check_vma=False,
    )
```

profile of v0, /device:TPU:0, one launch (start us, length us, event | category | flops | bytes accessed | tf_op | source)
XLA Modules:
  0.0 495.5 jit_solution(17342932502256121510)
XLA Ops:
  7.2 0.0 all-gather.2.cloned.1.call-start
  7.2 0.9 select_reduce_fusion.3
  8.1 0.1 convert_reduce_fusion.1
  8.3 0.1 fusion.20
  8.4 0.2 select_reduce_fusion.2
  8.6 0.7 fusion.21
  9.3 0.1 concatenate.9
  9.3 0.1 copy.122
  9.5 1.9 fusion.14
  11.3 0.0 all-gather.2.cloned.1.call-update
  11.3 0.0 reduce-scatter.4.cloned.1.call-start
  11.4 119.7 %all-gather.2.cloned.1.call-done = bf16[2048,4224]{1,0:T(8,128)(2,1)} async-done(((bf16[64,4224]{1,0:T(8,128)(2,1)}), bf16[2048,4224]{1,0:T(8,128)(2,1)}) %all-gather.2.cloned.1.call-update) | async-done | bytes 17301520 | tf_op jit(solution)/shard_map/all_gather | solution.py:39
  131.1 1.1 slice.44
  132.2 0.2 copy.116
  132.5 1.2 convert_reduce_fusion
  133.6 9.0 %fusion.6 = bf16[8,256,2048]{2,1,0:T(8,128)(2,1)} fusion(bf16[8,256,256]{2,1,0:T(8,128)(2,1)S(1)} %convert_reduce_fusion, bf16[8,256,4224]{2,1,0:T(8,128)(2,1)} %bitcast.75), kind=kOutput, calls=%fused_computation.13 | convolution fusion | flops 2151677952 | bytes 17825792 | tf_op jit(solution)/shard_map/crt,ctd->crd/dot_general | solution.py:68
  142.6 9.0 %fusion.9 = bf16[8,256,2048]{2,1,0:T(8,128)(2,1)} fusion(bf16[8,256,256]{2,1,0:T(8,128)(2,1)S(1)} %convert_reduce_fusion, bf16[8,256,4224]{2,1,0:T(8,128)(2,1)} %bitcast.76), kind=kOutput, calls=%fused_computation.14 | convolution fusion | flops 2151677952 | bytes 17825792 | tf_op jit(solution)/shard_map/crt,ctd->crd/dot_general | solution.py:71
  151.7 8.3 %copy.96 = bf16[8,8,32,2048]{3,2,1,0:T(8,128)(2,1)} copy(bf16[8,8,32,2048]{3,2,0,1:T(8,128)(2,1)} %bitcast.69) | data formatting | bytes 16777216 | tf_op jit(solution)/shard_map/transpose | solution.py:59
  160.0 8.2 %fusion.24 = f32[8,256,192]{1,2,0:T(8,128)S(1)} fusion(bf16[8,256,2048]{2,1,0:T(8,128)(2,1)} %bitcast.62, bf16[8,192,2048]{2,1,0:T(8,128)(2,1)} %param.12), kind=kOutput, calls=%fused_computation.58 | convolution fusion | flops 1610612736 | bytes 16252928 | tf_op jit(solution)/shard_map/erd,efd->erf/dot_general | solution.py:74
  168.2 0.0 copy-done
  168.2 0.0 copy-start.2
  168.2 7.6 %fusion.25 = f32[8,256,192]{1,2,0:T(8,128)} fusion(bf16[8,256,2048]{2,1,0:T(8,128)(2,1)S(1)} %bitcast.65, bf16[8,192,2048]{2,1,0:T(8,128)(2,1)} %param.13), kind=kOutput, calls=%fused_computation.59 | convolution fusion | flops 1610612736 | bytes 16252928 | tf_op jit(solution)/shard_map/erd,efd->erf/dot_general | solution.py:75
  175.8 19.6 %copy.102 = bf16[8,8,32,2048]{3,2,1,0:T(8,128)(2,1)} copy(bf16[8,8,32,2048]{3,2,0,1:T(8,128)(2,1)} %bitcast.68) | data formatting | bytes 16777216 | tf_op jit(solution)/shard_map/transpose | solution.py:59
  195.5 9.6 %multiply_reduce_fusion = (f32[8,256]{1,0:T(8,128)S(1)}, f32[8,256,192]{1,2,0:T(8,128)}) fusion(f32[8,256,192]{1,2,0:T(8,128)S(1)} %copy-done.3, f32[8,256,192]{1,2,0:T(8,128)S(1)} %fusion.24, bf16[8,256,2048]{2,1,0:T(8,128)(2,1)} %bitcast.72, bf16[8,192,2048]{2,1,0:T(8,128)(2,1)} %param.14), kind=kOutput, calls=%fused_computation.20 | convolution fusion | flops 1613363200 | bytes 19406848 | tf_op jit(solution)/shard_map/erd,efd->erf/dot_general | solution.py:76
  205.1 0.1 reshape.131
  205.2 0.1 broadcast_in_dim.68
  205.3 2.6 select_reduce_fusion.1
  207.9 0.1 reshape.124
  208.0 0.1 mul.75
  208.0 4.2 multiply_convert_fusion.2
  212.2 10.9 %fusion.26 = f32[8,256,2048]{2,1,0:T(8,128)} fusion(bf16[8,256,192]{1,2,0:T(8,128)(2,1)S(1)} %get-tuple-element.45, bf16[8,192,2048]{2,1,0:T(8,128)(2,1)} %param.12), kind=kOutput, calls=%fused_computation.60 | convolution fusion | flops 1610612736 | bytes 23855104 | tf_op jit(solution)/shard_map/erf,efd->erd/dot_general | solution.py:87
  223.1 13.5 %add_convert_fusion = bf16[8,256,2048]{2,1,0:T(8,128)(2,1)} fusion(f32[8,256,2048]{2,1,0:T(8,128)} %fusion.26, bf16[8,256,192]{1,2,0:T(8,128)(2,1)} %get-tuple-element.46, bf16[8,192,2048]{2,1,0:T(8,128)(2,1)} %param.13), kind=kOutput, calls=%fused_computation.3 | convolution fusion | flops 1619001344 | bytes 32243712 | tf_op jit(solution)/shard_map/erf,efd->erd/dot_general | solution.py:88
  236.6 8.4 %copy.103 = bf16[8,8,32,2048]{3,2,1,0:T(8,128)(2,1)} copy(bf16[8,8,32,2048]{3,2,0,1:T(8,128)(2,1)} %bitcast.77) | data formatting | bytes 16777216 | tf_op jit(solution)/shard_map/transpose | solution.py:64
  245.0 9.2 %convolution_convert_fusion.1 = bf16[8,256,2048]{2,1,0:T(8,128)(2,1)} fusion(bf16[8,256,256]{2,1,0:T(8,128)(2,1)S(1)} %convert_reduce_fusion, bf16[8,256,2048]{2,1,0:T(8,128)(2,1)} %bitcast.71), kind=kOutput, calls=%fused_computation.15 | convolution fusion | flops 2151677952 | bytes 17825792 | tf_op jit(solution)/shard_map/crt,crd->ctd/dot_general | solution.py:94
  254.2 5.7 %convolution_convert_fusion = bf16[8,256,2048]{2,1,0:T(8,128)(2,1)} fusion(bf16[8,256,192]{1,2,0:T(8,128)(2,1)S(1)} %get-tuple-element.44, bf16[8,192,2048]{2,1,0:T(8,128)(2,1)S(1)} %bitcast.79), kind=kOutput, calls=%fused_computation.12 | convolution fusion | flops 1614807040 | bytes 15466496 | tf_op jit(solution)/shard_map/erf,efd->erd/dot_general | solution.py:85
  259.9 8.4 %copy.99 = bf16[8,8,32,2048]{3,2,1,0:T(8,128)(2,1)} copy(bf16[8,8,32,2048]{3,2,0,1:T(8,128)(2,1)} %bitcast.67) | data formatting | bytes 16777216 | tf_op jit(solution)/shard_map/transpose | solution.py:64
  268.3 9.0 %convolution_convert_fusion.2 = bf16[8,256,2048]{2,1,0:T(8,128)(2,1)} fusion(bf16[8,256,256]{2,1,0:T(8,128)(2,1)S(1)} %convert_reduce_fusion, bf16[8,256,2048]{2,1,0:T(8,128)(2,1)} %bitcast.70), kind=kOutput, calls=%fused_computation.16 | convolution fusion | flops 2151677952 | bytes 17825792 | tf_op jit(solution)/shard_map/crt,crd->ctd/dot_general | solution.py:93
  277.3 0.3 copy.123
  277.6 13.9 %fusion.1 = bf16[8,256,4224]{2,1,0:T(8,128)(2,1)} fusion(bf16[8,256,4]{2,1,0:T(8,128)(2,1)S(1)} %copy.123, bf16[8,256,2048]{2,1,0:T(8,128)(2,1)} %convolution_convert_fusion.1, bf16[8,256,2048]{2,1,0:T(8,128)(2,1)} %convolution_convert_fusion.2), kind=kLoop, calls=%fused_computation.2 | loop fusion | flops 69206016 | bytes 34095104 | tf_op jit(solution)/shard_map/concatenate | solution.py:98
  291.5 0.0 reduce-scatter.4.cloned.1.call-update
  291.5 8.0 %convolution_convert_fusion.3 = bf16[8,192,2048]{2,1,0:T(8,128)(2,1)} fusion(bf16[8,256,192]{1,2,0:T(8,128)(2,1)S(1)} %get-tuple-element.44, bf16[8,256,2048]{2,1,0:T(8,128)(2,1)} %bitcast.73), kind=kOutput, calls=%fused_computation.17 | convolution fusion | flops 1613758464 | bytes 15466496 | tf_op jit(solution)/shard_map/erf,erd->efd/dot_general | solution.py:92
  299.5 8.5 %convolution_convert_fusion.4 = bf16[8,192,2048]{2,1,0:T(8,128)(2,1)} fusion(bf16[8,256,192]{1,2,0:T(8,128)(2,1)S(1)} %copy-done.1, bf16[8,256,2048]{2,1,0:T(8,128)(2,1)} %bitcast.63), kind=kOutput, calls=%fused_computation.18 | convolution fusion | flops 1613758464 | bytes 15466496 | tf_op jit(solution)/shard_map/erf,erd->efd/dot_general | solution.py:91
  308.0 8.5 %convolution_convert_fusion.5 = bf16[8,192,2048]{2,1,0:T(8,128)(2,1)} fusion(bf16[8,256,192]{1,2,0:T(8,128)(2,1)S(1)} %get-tuple-element.45, bf16[8,256,2048]{2,1,0:T(8,128)(2,1)} %bitcast.64), kind=kOutput, calls=%fused_computation.19 | convolution fusion | flops 1613758464 | bytes 15466496 | tf_op jit(solution)/shard_map/erf,erd->efd/dot_general | solution.py:90
  316.5 168.5 %reduce-scatter.4.cloned.1.call-done = bf16[64,4224]{1,0:T(8,128)(2,1)} async-done(((bf16[2048,4224]{1,0:T(8,128)(2,1)}), bf16[64,4224]{1,0:T(8,128)(2,1)}) %reduce-scatter.4.cloned.1.call-update) | async-done | bytes 540688
  485.0 0.7 slice.54
  485.8 0.1 copy.121
  485.8 0.6 convert_element_type.108
  486.4 1.9 fusion.23
  (21 shorter events, 0.1 us)
Async XLA Ops:
  7.2 123.9 %all-gather.2.cloned.1.call-start = ((), (), s32[]{:S(2)}) async-start(), calls=%async_computation.1 | async-start | bytes 17842176 | tf_op jit(solution)/shard_map/all_gather | solution.py:39
  11.3 473.7 %reduce-scatter.4.cloned.1.call-start = ((), (), s32[]{:S(2)}) async-start(), calls=%async_computation.2 | async-start | bytes 17842176
  160.0 8.2 %copy-start = (bf16[8,8,32,2048]{3,2,1,0:T(8,128)(2,1)S(1)}, bf16[8,8,32,2048]{3,2,1,0:T(8,128)(2,1)}, u32[]{:S(2)}) copy-start(bf16[8,8,32,2048]{3,2,1,0:T(8,128)(2,1)} %copy.96) | copy-start | bytes 25165828
  168.2 27.3 %copy-start.2 = (f32[8,256,192]{1,2,0:T(8,128)}, f32[8,256,192]{1,2,0:T(8,128)S(1)}, u32[]{:S(2)}) copy-start(f32[8,256,192]{1,2,0:T(8,128)S(1)} %fusion.24) | copy-start | bytes 4718596
  175.8 19.7 %copy-start.3 = (f32[8,256,192]{1,2,0:T(8,128)S(1)}, f32[8,256,192]{1,2,0:T(8,128)}, u32[]{:S(2)}) copy-start(f32[8,256,192]{1,2,0:T(8,128)} %fusion.25) | copy-start | bytes 4718596
  236.6 17.6 %slice-start = ((s8[6291456]{0:T(1024)(128)(4,1)}), s8[2097152]{0:T(1024)(128)(4,1)S(1)}, s32[]{:S(2)}) async-start(s8[6291456]{0:T(1024)(128)(4,1)} %bitcast.78), calls=%async_computation.3 | async-start | bytes 4194304
  245.0 9.2 %slice-start.1 = ((s8[6291456]{0:T(1024)(128)(4,1)}), s8[4194304]{0:T(1024)(128)(4,1)S(1)}, s32[]{:S(2)}) async-start(s8[6291456]{0:T(1024)(128)(4,1)} %bitcast.78), calls=%async_computation.4 | async-start | bytes 8388608
  291.5 8.0 %copy-start.1 = (bf16[8,256,192]{1,2,0:T(8,128)(2,1)S(1)}, bf16[8,256,192]{1,2,0:T(8,128)(2,1)}, u32[]{:S(2)}) copy-start(bf16[8,256,192]{1,2,0:T(8,128)(2,1)} %get-tuple-element.46) | copy-start | bytes 2359300
Sparse Core Ops, SparseCore 0:
  11.5 119.5 all-gather.1
  291.6 193.3 reduce-scatter.3
where the time goes:
time: 505 us; the launch traced here: 496 us
  waiting for transfers between devices  288 us (57%)
  matrix products  117 us (23%)
  local copies, waits for them, and re-layouts  49.7 us (10%)
  other arithmetic  26.3 us (5%)
  between operations  14.5 us (3%)
    unnamed x3, waiting for transfers between devices  169 us
    all_gather x1, waiting for transfers between devices, per_device(): allp = lax.all_gather(packed, AXES, axis=0, tiled=True)  120 us
    transpose x3, local copies, waits for them, and re-layouts, to_expert(): v = jnp.swapaxes(v, 0, 1)  28 us
    transpose x3, local copies, waits for them, and re-layouts, to_chunk(): v = jnp.swapaxes(v, 0, 1)  16.9 us
    concatenate x1, other arithmetic, per_device(): jnp.concatenate([part_m.astype(BF16), part_b.astype(BF16), part_g.astype(...  13.9 us
    dot_general x1, matrix products, per_device(): jnp.einsum('erf,efd->erd', grad_up, w_up, preferred_element_type=F32)  13.5 us
    dot_general x1, matrix products, per_device(): jnp.einsum('erf,efd->erd', grad_gate, w_gate, preferred_element_type=F32)  10.9 us
  transfers between devices with their start and end apart: 2, of which 2 were waited for; matrix products, arithmetic and copies ran while one was open for 5% of the time, Pallas kernels for 0%

commit v1 on v0

--- a/solution.py
+++ b/solution.py
@@ -8,6 +8,18 @@
 F32 = jnp.float32
 BF16 = jnp.bfloat16
 AXES = ("dp", "expert")
+
+
+def collect(x, axis, dim):
+    ways, here, step = (lax.axis_size(axis), lax.axis_index(axis), x.shape[dim])
+    line, have = (x, 1)
+    while have < ways:
+        line = jnp.concatenate(
+            [line, lax.ppermute(line, axis, [(d, (d - have) % ways) for d in range(ways)])],
+            axis=dim,
+        )
+        have = 2 * have
+    return jnp.roll(line, here * step, axis=dim)
 
 
 def split3(v):
@@ -36,7 +48,7 @@
     extra = jnp.concatenate([slot.astype(BF16), pos.astype(BF16), g1, g2, g3], axis=1)
     extra = jnp.pad(extra, ((0, 0), (0, PAD - extra.shape[1])))
     packed = jnp.concatenate([tokens, cotangent, extra], axis=1)
-    allp = lax.all_gather(packed, AXES, axis=0, tiled=True)
+    allp = collect(packed, AXES, 0)
     allp = allp.reshape(chunks, blocks * tok, 2 * width + PAD)
     x_all = allp[:, :, :width]
     c_all = allp[:, :, width : 2 * width]

time: 505 us -> 809 us (1.60)
  waiting for transfers between devices: 288 us -> 540 us
  local copies, waits for them, and re-layouts: 49.7 us -> 83.2 us
  starting transfers between devices: 0.08 us -> 9.08 us
    ppermute x0 -> x5, waiting for transfers between devices: none -> 362 us  [collect(): lax.ppermute(line, axis, [(d, (d - have) % ways) for d in range(ways)])]
    all_gather x1 -> x0, waiting for transfers between devices: 120 us -> none  [per_device(): allp = lax.all_gather(packed, AXES, axis=0, tiled=True)]
    unnamed x16 -> x42, local copies, waits for them, and re-layouts: 0.78 us -> 26.9 us
    transpose x3, local copies, waits for them, and re-layouts: 28 us -> 16.6 us  [to_expert(): v = jnp.swapaxes(v, 0, 1)]
    concatenate x0 -> x2, local copies, waits for them, and re-layouts: none -> 11.3 us  [the longest x1 7.38 us: collect(): return jnp.roll(line, here * step, axis=dim)]
    dot_general x1, matrix products: 7.62 us -> 18.9 us  [per_device(): jnp.einsum('erd,efd->erf', x_rows, w_up, preferred_element_type=F32)]
    unnamed x3 -> x2, waiting for transfers between devices: 169 us -> 178 us
    ppermute x0 -> x5, starting transfers between devices: none -> 9.04 us  [collect(): lax.ppermute(line, axis, [(d, (d - have) % ways) for d in range(ways)])]
  transfers between devices with their start and end apart: 2 -> 6, of which waited for: 2 -> 6; matrix products, arithmetic and copies ran while one was open for 5% -> 3% of each run, Pallas kernels for 0% -> 0%
where the time goes in v1:
time: 809 us; the launch traced here: 804 us
  waiting for transfers between devices  540 us (67%)
  matrix products  125 us (15%)
  local copies, waits for them, and re-layouts  83.2 us (10%)
  other arithmetic  32.1 us (4%)
  between operations  14.5 us (2%)
  starting transfers between devices  9.08 us (1%)
    ppermute x5, waiting for transfers between devices, collect(): lax.ppermute(line, axis, [(d, (d - have) % ways) for d in range(ways)])  362 us
    unnamed x2, waiting for transfers between devices  178 us
    unnamed x42, local copies, waits for them, and re-layouts  26.9 us
    dot_general x1, matrix products, per_device(): jnp.einsum('erd,efd->erf', x_rows, w_up, preferred_element_type=F32)  18.9 us
    transpose x3, local copies, waits for them, and re-layouts, to_chunk(): v = jnp.swapaxes(v, 0, 1)  16.9 us
    transpose x3, local copies, waits for them, and re-layouts, to_expert(): v = jnp.swapaxes(v, 0, 1)  16.6 us
  transfers between devices with their start and end apart: 6, of which 6 were waited for; matrix products, arithmetic and copies ran while one was open for 3% of the time, Pallas kernels for 0%

profile of v1, /device:TPU:0, one launch (start us, length us, event | category | flops | bytes accessed | tf_op | source)
XLA Modules:
  0.0 803.5 jit_solution(7608984896195848699)
XLA Ops:
  7.2 1.0 select_reduce_fusion.3
  9.5 2.1 constant_dynamic-update-slice_fusion.4
  11.7 6.4 collective-permute-start
  18.1 11.7 %collective-permute-done = bf16[64,4224]{1,0:T(8,128)(2,1)S(1)} collective-permute-done((bf16[64,4224]{1,0:T(8,128)(2,1)S(1)}, bf16[64,4224]{1,0:T(8,128)(2,1)S(1)}, u32[]{:S(2)}, u32[]{:S(2)}) %collective-permute-start) | collective-permute-done | bytes 540704 | tf_op jit(solution)/shard_map/ppermute | solution.py:18
  29.8 1.3 pad_maximum_fusion.2
  31.6 24.5 %collective-permute-done.1 = bf16[128,4224]{1,0:T(8,128)(2,1)S(1)} collective-permute-done((bf16[128,4224]{1,0:T(8,128)(2,1)S(1)}, bf16[128,4224]{1,0:T(8,128)(2,1)S(1)}, u32[]{:S(2)}, u32[]{:S(2)}) %collective-permute-start.1) | collective-permute-done | bytes 1081376 | tf_op jit(solution)/shard_map/ppermute | solution.py:18
  56.1 1.2 pad_maximum_fusion.1
  57.4 95.9 %collective-permute-done.2 = bf16[256,4224]{1,0:T(8,128)(2,1)S(1)} collective-permute-done((bf16[256,4224]{1,0:T(8,128)(2,1)S(1)}, bf16[256,4224]{1,0:T(8,128)(2,1)S(1)}, u32[]{:S(2)}, u32[]{:S(2)}) %collective-permute-start.2) | collective-permute-done | bytes 2162720 | tf_op jit(solution)/shard_map/ppermute | solution.py:18
  153.3 2.2 pad_maximum_fusion
  156.3 1.1 constant_dynamic-update-slice_fusion.3
  157.4 1.5 constant_dynamic-update-slice_fusion.2
  158.8 2.3 constant_dynamic-update-slice_fusion.1
  161.2 42.5 %collective-permute-done.3 = bf16[512,4224]{1,0:T(8,128)(2,1)S(1)} collective-permute-done((bf16[512,4224]{1,0:T(8,128)(2,1)S(1)}, bf16[512,4224]{1,0:T(8,128)(2,1)S(1)}, u32[]{:S(2)}, u32[]{:S(2)}) %collective-permute-start.3) | collective-permute-done | bytes 4325408 | tf_op jit(solution)/shard_map/ppermute | solution.py:18
  203.7 2.1 copy-done.2
  205.8 3.9 constant_dynamic-update-slice_fusion
  209.7 1.3 collective-permute-start.4
  211.0 187.4 %collective-permute-done.4 = bf16[1024,4224]{1,0:T(8,128)(2,1)} collective-permute-done((bf16[1024,4224]{1,0:T(8,128)(2,1)}, bf16[1024,4224]{1,0:T(8,128)(2,1)}, u32[]{:S(2)}, u32[]{:S(2)}) %collective-permute-start.4) | collective-permute-done | bytes 8650784 | tf_op jit(solution)/shard_map/ppermute | solution.py:18
  398.4 7.4 constant_dynamic-update-slice_fusion.11
  406.7 0.9 constant_dynamic-update-slice_fusion.9
  407.5 1.1 constant_dynamic-update-slice_fusion.8
  408.6 1.5 constant_dynamic-update-slice_fusion.7
  410.1 2.3 constant_dynamic-update-slice_fusion.6
  412.5 7.4 constant_dynamic-update-slice_fusion.5
  419.9 8.5 %constant_dynamic-slice_fusion = bf16[2048,4224]{1,0:T(8,128)(2,1)S(1)} fusion(bf16[4096,4224]{1,0:T(8,128)(2,1)} %constant_dynamic-update-slice_fusion.5, s32[]{:T(128)S(6)} %select_n.49), kind=kLoop, calls=%fused_computation.75 | loop fusion | bytes 34603012 | tf_op jit(solution)/shard_map/jit(_roll_dynamic)/dynamic_slice | solution.py:22
  428.3 5.9 copy-done.1
  434.7 1.2 convert_reduce_fusion
  435.8 9.0 %fusion.9 = bf16[8,256,2048]{2,1,0:T(8,128)(2,1)} fusion(bf16[8,256,256]{2,1,0:T(8,128)(2,1)S(1)} %convert_reduce_fusion, bf16[8,256,4224]{2,1,0:T(8,128)(2,1)} %bitcast.69), kind=kOutput, calls=%fused_computation.14 | convolution fusion | flops 2151677952 | bytes 17825792 | tf_op jit(solution)/shard_map/crt,ctd->crd/dot_general | solution.py:83
  444.9 9.0 %fusion.6 = bf16[8,256,2048]{2,1,0:T(8,128)(2,1)} fusion(bf16[8,256,256]{2,1,0:T(8,128)(2,1)S(1)} %convert_reduce_fusion, bf16[8,256,4224]{2,1,0:T(8,128)(2,1)} %bitcast.70), kind=kOutput, calls=%fused_computation.13 | convolution fusion | flops 2151677952 | bytes 17825792 | tf_op jit(solution)/shard_map/crt,ctd->crd/dot_general | solution.py:80
  453.9 8.3 %copy.102 = bf16[8,8,32,2048]{3,2,1,0:T(8,128)(2,1)} copy(bf16[8,8,32,2048]{3,2,0,1:T(8,128)(2,1)} %bitcast.74) | data formatting | bytes 16777216 | tf_op jit(solution)/shard_map/transpose | solution.py:71
  462.2 8.3 %copy.96 = bf16[8,8,32,2048]{3,2,1,0:T(8,128)(2,1)} copy(bf16[8,8,32,2048]{3,2,0,1:T(8,128)(2,1)} %bitcast.73) | data formatting | bytes 16777216 | tf_op jit(solution)/shard_map/transpose | solution.py:71
  470.5 8.2 %fusion.22 = f32[8,256,192]{1,2,0:T(8,128)S(1)} fusion(bf16[8,256,2048]{2,1,0:T(8,128)(2,1)} %bitcast.62, bf16[8,192,2048]{2,1,0:T(8,128)(2,1)} %param.12), kind=kOutput, calls=%fused_computation.77 | convolution fusion | flops 1610612736 | bytes 16252928 | tf_op jit(solution)/shard_map/erd,efd->erf/dot_general | solution.py:86
  478.7 18.9 %fusion.23 = f32[8,256,192]{1,2,0:T(8,128)} fusion(bf16[8,256,2048]{2,1,0:T(8,128)(2,1)S(1)} %bitcast.64, bf16[8,192,2048]{2,1,0:T(8,128)(2,1)} %param.13), kind=kOutput, calls=%fused_computation.78 | convolution fusion | flops 1610612736 | bytes 16252928 | tf_op jit(solution)/shard_map/erd,efd->erf/dot_general | solution.py:87
  497.7 10.0 %multiply_reduce_fusion = (f32[8,256]{1,0:T(8,128)S(1)}, f32[8,256,192]{1,2,0:T(8,128)}) fusion(f32[8,256,192]{1,2,0:T(8,128)} %fusion.23, f32[8,256,192]{1,2,0:T(8,128)S(1)} %fusion.22, bf16[8,256,2048]{2,1,0:T(8,128)(2,1)} %bitcast.77, bf16[8,192,2048]{2,1,0:T(8,128)(2,1)} %param.14), kind=kOutput, calls=%fused_computation.22 | convolution fusion | flops 1613363200 | bytes 19406848 | tf_op jit(solution)/shard_map/erd,efd->erf/dot_general | solution.py:88
  507.8 2.6 select_reduce_fusion.1
  510.6 4.2 multiply_convert_fusion.2
  514.8 8.4 %convolution_convert_fusion = bf16[8,256,2048]{2,1,0:T(8,128)(2,1)} fusion(bf16[8,256,192]{1,2,0:T(8,128)(2,1)S(1)} %get-tuple-element.46, bf16[8,192,2048]{2,1,0:T(8,128)(2,1)} %param.14), kind=kOutput, calls=%fused_computation.12 | convolution fusion | flops 1614807040 | bytes 15466496 | tf_op jit(solution)/shard_map/erf,efd->erd/dot_general | solution.py:97
  523.2 8.4 %copy.99 = bf16[8,8,32,2048]{3,2,1,0:T(8,128)(2,1)} copy(bf16[8,8,32,2048]{3,2,0,1:T(8,128)(2,1)} %bitcast.72) | data formatting | bytes 16777216 | tf_op jit(solution)/shard_map/transpose | solution.py:76
  531.6 9.2 %convolution_convert_fusion.2 = bf16[8,256,2048]{2,1,0:T(8,128)(2,1)} fusion(bf16[8,256,256]{2,1,0:T(8,128)(2,1)S(1)} %convert_reduce_fusion, bf16[8,256,2048]{2,1,0:T(8,128)(2,1)} %bitcast.76), kind=kOutput, calls=%fused_computation.16 | convolution fusion | flops 2151677952 | bytes 17825792 | tf_op jit(solution)/shard_map/crt,crd->ctd/dot_general | solution.py:105
  540.8 8.2 %fusion.24 = f32[8,256,2048]{2,1,0:T(8,128)} fusion(bf16[8,256,192]{1,2,0:T(8,128)(2,1)S(1)} %get-tuple-element.47, bf16[8,192,2048]{2,1,0:T(8,128)(2,1)S(1)} %bitcast.81), kind=kOutput, calls=%fused_computation.79 | convolution fusion | flops 1610612736 | bytes 23855104 | tf_op jit(solution)/shard_map/erf,efd->erd/dot_general | solution.py:99
  548.9 13.5 %add_convert_fusion = bf16[8,256,2048]{2,1,0:T(8,128)(2,1)} fusion(f32[8,256,2048]{2,1,0:T(8,128)} %fusion.24, bf16[8,256,192]{1,2,0:T(8,128)(2,1)} %get-tuple-element.48, bf16[8,192,2048]{2,1,0:T(8,128)(2,1)} %param.13), kind=kOutput, calls=%fused_computation.3 | convolution fusion | flops 1619001344 | bytes 32243712 | tf_op jit(solution)/shard_map/erf,efd->erd/dot_general | solution.py:100
  562.4 8.4 %copy.103 = bf16[8,8,32,2048]{3,2,1,0:T(8,128)(2,1)} copy(bf16[8,8,32,2048]{3,2,0,1:T(8,128)(2,1)} %bitcast.79) | data formatting | bytes 16777216 | tf_op jit(solution)/shard_map/transpose | solution.py:76
  570.9 9.0 %convolution_convert_fusion.1 = bf16[8,256,2048]{2,1,0:T(8,128)(2,1)} fusion(bf16[8,256,256]{2,1,0:T(8,128)(2,1)S(1)} %convert_reduce_fusion, bf16[8,256,2048]{2,1,0:T(8,128)(2,1)} %bitcast.75), kind=kOutput, calls=%fused_computation.15 | convolution fusion | flops 2151677952 | bytes 17825792 | tf_op jit(solution)/shard_map/crt,crd->ctd/dot_general | solution.py:106
  580.2 13.8 %fusion.1 = bf16[8,256,4224]{2,1,0:T(8,128)(2,1)} fusion(bf16[8,256,4]{2,1,0:T(8,128)(2,1)S(1)} %copy.123, bf16[8,256,2048]{2,1,0:T(8,128)(2,1)} %convolution_convert_fusion.1, bf16[8,256,2048]{2,1,0:T(8,128)(2,1)} %convolution_convert_fusion.2), kind=kLoop, calls=%fused_computation.2 | loop fusion | flops 69206016 | bytes 34095104 | tf_op jit(solution)/shard_map/concatenate | solution.py:110
  594.1 8.1 %convolution_convert_fusion.3 = bf16[8,192,2048]{2,1,0:T(8,128)(2,1)} fusion(bf16[8,256,192]{1,2,0:T(8,128)(2,1)S(1)} %get-tuple-element.46, bf16[8,256,2048]{2,1,0:T(8,128)(2,1)} %bitcast.78), kind=kOutput, calls=%fused_computation.17 | convolution fusion | flops 1613758464 | bytes 15466496 | tf_op jit(solution)/shard_map/erf,erd->efd/dot_general | solution.py:104
  602.2 8.8 %convolution_convert_fusion.4 = bf16[8,192,2048]{2,1,0:T(8,128)(2,1)} fusion(bf16[8,256,192]{1,2,0:T(8,128)(2,1)S(1)} %copy-done.6, bf16[8,256,2048]{2,1,0:T(8,128)(2,1)} %bitcast.63), kind=kOutput, calls=%fused_computation.18 | convolution fusion | flops 1613758464 | bytes 15466496 | tf_op jit(solution)/shard_map/erf,erd->efd/dot_general | solution.py:103
  610.9 4.5 convolution_convert_fusion.5
  615.5 177.7 %reduce-scatter.4.cloned.1.call-done = bf16[64,4224]{1,0:T(8,128)(2,1)} async-done(((bf16[2048,4224]{1,0:T(8,128)(2,1)}), bf16[64,4224]{1,0:T(8,128)(2,1)}) %reduce-scatter.4.cloned.1.call-update) | async-done | bytes 540688
  794.6 1.9 fusion.21
  (63 shorter events, 6.1 us)
Async XLA Ops:
  7.2 146.1 %copy-start.7 = (bf16[64,2048]{1,0:T(8,128)(2,1)S(1)}, bf16[64,2048]{1,0:T(8,128)(2,1)}, u32[]{:S(2)}) copy-start(bf16[64,2048]{1,0:T(8,128)(2,1)} %param.15) | copy-start | bytes 786436
  7.2 786.0 %reduce-scatter.4.cloned.1.call-start = ((), (), s32[]{:S(2)}) async-start(), calls=%async_computation.1 | async-start | bytes 17842176
  9.5 143.8 %copy-start.8 = (bf16[64,2048]{1,0:T(8,128)(2,1)S(1)}, bf16[64,2048]{1,0:T(8,128)(2,1)}, u32[]{:S(2)}) copy-start(bf16[64,2048]{1,0:T(8,128)(2,1)} %param.8) | copy-start | bytes 786436
  11.7 18.1 %collective-permute-start = (bf16[64,4224]{1,0:T(8,128)(2,1)S(1)}, bf16[64,4224]{1,0:T(8,128)(2,1)S(1)}, u32[]{:S(2)}, u32[]{:S(2)}) collective-permute-start(bf16[64,4224]{1,0:T(8,128)(2,1)S(1)} %get-tuple-element.59), channel_id=1, source_target_pairs={{0,31},{1,0},{2,1},{3,2},{4,3},{5,4},{6,5},{7,6},{8,7},{9,8},{10,9... | collective-permute-start | bytes 1622024 | tf_op jit(solution)/shard_map/ppermute | solution.py:18
  29.8 129.1 %copy-start.4 = (bf16[64,4224]{1,0:T(8,128)(2,1)}, bf16[64,4224]{1,0:T(8,128)(2,1)S(1)}, u32[]{:S(2)}) copy-start(bf16[64,4224]{1,0:T(8,128)(2,1)S(1)} %collective-permute-done) | copy-start | bytes 1622020
  31.1 25.0 %collective-permute-start.1 = (bf16[128,4224]{1,0:T(8,128)(2,1)S(1)}, bf16[128,4224]{1,0:T(8,128)(2,1)S(1)}, u32[]{:S(2)}, u32[]{:S(2)}) collective-permute-start(bf16[128,4224]{1,0:T(8,128)(2,1)S(1)} %pad_maximum_fusion.2), channel_id=1, source_target_pairs={{0,30},{1,31},{2,0},{3,1},{4,2},{5,3},{6,4},{7,5},{8,6},{9,7},{10,... | collective-permute-start | bytes 3244040 | tf_op jit(solution)/shard_map/ppermute | solution.py:18
  57.3 96.0 %collective-permute-start.2 = (bf16[256,4224]{1,0:T(8,128)(2,1)S(1)}, bf16[256,4224]{1,0:T(8,128)(2,1)S(1)}, u32[]{:S(2)}, u32[]{:S(2)}) collective-permute-start(bf16[256,4224]{1,0:T(8,128)(2,1)S(1)} %pad_maximum_fusion.1), channel_id=1, source_target_pairs={{0,28},{1,29},{2,30},{3,31},{4,0},{5,1},{6,2},{7,3},{8,4},{9,5},{1... | collective-permute-start | bytes 6488072 | tf_op jit(solution)/shard_map/ppermute | solution.py:18
  155.5 48.2 %collective-permute-start.3 = (bf16[512,4224]{1,0:T(8,128)(2,1)S(1)}, bf16[512,4224]{1,0:T(8,128)(2,1)S(1)}, u32[]{:S(2)}, u32[]{:S(2)}) collective-permute-start(bf16[512,4224]{1,0:T(8,128)(2,1)S(1)} %pad_maximum_fusion), channel_id=1, source_target_pairs={{0,24},{1,25},{2,26},{3,27},{4,28},{5,29},{6,30},{7,31},{8,0},{9,1... | collective-permute-start | bytes 12976136 | tf_op jit(solution)/shard_map/ppermute | solution.py:18
  203.7 2.1 copy-start.2
  209.7 188.7 %collective-permute-start.4 = (bf16[1024,4224]{1,0:T(8,128)(2,1)}, bf16[1024,4224]{1,0:T(8,128)(2,1)}, u32[]{:S(2)}, u32[]{:S(2)}) collective-permute-start(bf16[1024,4224]{1,0:T(8,128)(2,1)} %get-tuple-element.44), channel_id=1, source_target_pairs={{0,16},{1,17},{2,18},{3,19},{4,20},{5,21},{6,22},{7,23},{8,24},{9,... | collective-permute-start | bytes 25952264 | tf_op jit(solution)/shard_map/ppermute | solution.py:18
  398.4 7.5 copy-start.9
  398.4 8.3 %copy-start.5 = (bf16[64,4224]{1,0:T(8,128)(2,1)S(1)}, bf16[64,4224]{1,0:T(8,128)(2,1)}, u32[]{:S(2)}) copy-start(bf16[64,4224]{1,0:T(8,128)(2,1)} %copy-done.4) | copy-start | bytes 1622020
  405.8 4.3 copy-start.3
  428.3 5.9 copy-start.1
  470.5 8.2 %copy-start = (bf16[8,8,32,2048]{3,2,1,0:T(8,128)(2,1)S(1)}, bf16[8,8,32,2048]{3,2,1,0:T(8,128)(2,1)}, u32[]{:S(2)}) copy-start(bf16[8,8,32,2048]{3,2,1,0:T(8,128)(2,1)} %copy.96) | copy-start | bytes 25165828
  478.7 18.9 %copy-start.10 = (f32[8,256,192]{1,2,0:T(8,128)}, f32[8,256,192]{1,2,0:T(8,128)S(1)}, u32[]{:S(2)}) copy-start(f32[8,256,192]{1,2,0:T(8,128)S(1)} %fusion.22) | copy-start | bytes 4718596
  523.2 17.6 %slice-start.2 = ((s8[6291456]{0:T(1024)(128)(4,1)}), s8[2097152]{0:T(1024)(128)(4,1)S(1)}, s32[]{:S(2)}) async-start(s8[6291456]{0:T(1024)(128)(4,1)} %bitcast.80), calls=%async_computation.4 | async-start | bytes 4194304
  531.6 9.2 %slice-start.3 = ((s8[6291456]{0:T(1024)(128)(4,1)}), s8[4194304]{0:T(1024)(128)(4,1)S(1)}, s32[]{:S(2)}) async-start(s8[6291456]{0:T(1024)(128)(4,1)} %bitcast.80), calls=%async_computation.5 | async-start | bytes 8388608
  594.1 8.1 %copy-start.6 = (bf16[8,256,192]{1,2,0:T(8,128)(2,1)S(1)}, bf16[8,256,192]{1,2,0:T(8,128)(2,1)}, u32[]{:S(2)}) copy-start(bf16[8,256,192]{1,2,0:T(8,128)(2,1)} %get-tuple-element.48) | copy-start | bytes 2359300
  594.1 16.8 %slice-start = ((s8[8388608]{0:T(1024)(128)(4,1)}), s8[4194304]{0:T(1024)(128)(4,1)S(1)}, s32[]{:S(2)}) async-start(s8[8388608]{0:T(1024)(128)(4,1)} %bitcast.65), calls=%async_computation.2 | async-start | bytes 8388608
  602.2 8.8 %slice-start.1 = ((s8[8388608]{0:T(1024)(128)(4,1)}), s8[4194304]{0:T(1024)(128)(4,1)S(1)}, s32[]{:S(2)}) async-start(s8[8388608]{0:T(1024)(128)(4,1)} %bitcast.65), calls=%async_computation.3 | async-start | bytes 8388608
Sparse Core Ops, SparseCore 0:
  594.2 198.9 reduce-scatter.3
